TPU v7x, 256 devices: a whole 4x4x8 slice. The times are simulated.
256 devices in a mesh: batch: 2 (over x_hi), head: 8 (over y, x_lo), blk: 16 (over z, core).
Axes of the slice: x: 4 (x_hi: 2, x_lo: 2; x = x_hi * 2 + x_lo), y: 4, z: 8, core: 2. Of those that a mesh axis runs over, the one named last changes fastest.
Arguments:
- tokens: bfloat16 [32, 2048, 1024], P(('batch', 'blk'), 'head'), parts along dimension 0, may hold values from -10.5 to 10.5
- proj_weight: bfloat16 [1024, 3072], replicated, may hold values from -0.1875 to 0.1875
- out_weight: bfloat16 [1024, 1024], replicated, may hold values from -1.5 to 1.5
- pattern: int32 [512, 16], P(('batch', 'blk')), parts along dimension 0, may hold values from 0 to 255, as said below
Outputs:
- mixed_out: bfloat16 [32, 2048, 1024], P(('batch', 'blk'), 'head'), parts along dimension 0
There are 2 independent parts, one for each index of `batch`. A program takes and returns all parts, laid end to end along the dimension named above; an argument that names none is the same for every part. Nothing has to cross between parts.
Inputs may be any that keep to these rules, and one draw needn't show every extreme that they name: `pattern`: row i lists first 6 distinct blocks j with |j - i| <= 8, among them i itself, then 10 distinct summary blocks j (j % 16 >= 12) with |j - i| > 8. Every row with 8 <= i < 248 lists i - 8 and i + 8.
All inputs are finite; a program needn't handle non-finite values.
Results may differ from a plain program's by a relative error of at most 0.0095.
Values may be sent and summed in bfloat16 or wider, within the bound.
A program may use at most 128 MiB of HBM per device.

v0:
```python
import jax
import jax.numpy as jnp
from jax import lax
from jax.sharding import PartitionSpec as P

D = 1024
H = 16
HD = 64
BLK = 128
TOK_DEV = 2048
SB = 16
KSEL = 16


def on_device(tokens, proj_weight, out_weight, pattern):
    heads_axis = lax.axis_size("head")
    local_heads = H // heads_axis
    head_width = local_heads * HD
    col_width = local_heads * 3 * HD
    own_rows = tokens[0]
    local_tokens = own_rows.shape[0]
    start_col = lax.axis_index("head") * col_width
    columns = lax.dynamic_slice_in_dim(proj_weight, start_col, col_width, 1)
    columns = columns.reshape(D, local_heads, 3, HD).transpose(0, 2, 1, 3).reshape(D, col_width)
    projected = jnp.dot(
        lax.all_gather(own_rows, "head", axis=0, tiled=True),
        columns,
        preferred_element_type=jnp.float32,
    ).astype(jnp.bfloat16)
    queries = projected[:, :head_width]
    key_value = projected[:, head_width:]
    source = lax.all_gather(key_value, "blk", axis=0, tiled=True)
    source_blocks = source.reshape(-1, BLK, 2 * head_width)
    group_size = 4
    group_count = SB // group_size
    query_groups = queries.reshape(group_count, group_size, BLK, head_width)
    position_groups = pattern.reshape(group_count, group_size, KSEL)
    score_scale = HD ** (-0.5)
    lane_head = lax.broadcasted_iota(jnp.int32, (1, 1, head_width), 2) // HD

    def attend(operands):
        query_group, positions = operands
        picked = source_blocks[positions].reshape(group_size, KSEL * BLK, 2 * head_width)
        key_rows = picked[:, :, :head_width]
        value_rows = picked[:, :, head_width:]
        total = jnp.zeros((group_size, BLK, head_width), jnp.float32)
        for which in range(local_heads):
            inside = lane_head == which
            masked = jnp.where(inside, query_group, jnp.zeros_like(query_group))
            scores = (
                jnp.einsum("gqc,gkc->gqk", masked, key_rows, preferred_element_type=jnp.float32)
                * score_scale
            )
            row_max = jnp.max(scores, axis=-1, keepdims=True)
            raised = jnp.exp(scores - row_max)
            weights = (raised / jnp.sum(raised, axis=-1, keepdims=True)).astype(jnp.bfloat16)
            product = jnp.einsum(
                "gqk,gkc->gqc", weights, value_rows, preferred_element_type=jnp.float32
            )
            total = total + jnp.where(inside, product, 0.0)
        return total.astype(jnp.bfloat16)

    attended = lax.map(attend, (query_groups, position_groups))
    attended = attended.reshape(TOK_DEV, head_width)
    token_heads = lax.all_to_all(attended, "head", split_axis=0, concat_axis=1, tiled=True)
    mixed_out = jnp.dot(token_heads, out_weight, preferred_element_type=jnp.float32).astype(
        jnp.bfloat16
    )
    return mixed_out.reshape(1, local_tokens, D)


def solution(mesh):
    return jax.shard_map(
        on_device,
        mesh=mesh,
        in_specs=(P(("batch", "blk"), "head", None), P(), P(), P(("batch", "blk"), None)),
        out_specs=P(("batch", "blk"), "head", None),
        check_vma=False,
    )
```

profile of v0, /device:TPU:1, one launch (start us, length us, event | category | flops | bytes accessed | tf_op | source)
XLA Modules:
  0.0 347.2 jit_solution(8824220184311968826)
XLA Ops:
  7.3 1.2 constant_dynamic-slice_fusion
  8.5 1.2 copy.18
  9.7 1.2 copy.12
  10.9 95.1 %all-gather.6.cloned.1.call-done = bf16[1,2048,1024]{2,1,0:T(8,128)(2,1)} async-done(((bf16[1,256,1024]{2,1,0:T(8,128)(2,1)}), bf16[1,2048,1024]{2,1,0:T(8,128)(2,1)}) %all-gather.6.cloned.1.call-update) | async-done | bytes 4194320 | tf_op jit(solution)/shard_map/all_gather | solution.py:26
  106.0 4.0 %fusion.111 = bf16[2048,384]{0,1:T(8,128)(2,1)S(1)} fusion(bf16[1024,384]{0,1:T(8,128)(2,1)S(1)} %bitcast.86, bf16[1,2048,1024]{2,1,0:T(8,128)(2,1)} %all-gather.6.cloned.1.call-done), kind=kOutput, calls=%fused_computation.67 | convolution fusion | flops 1611399168 | bytes 6553600 | tf_op jit(solution)/shard_map/dot_general | solution.py:25
  110.0 1.1 copy-done.1
  112.3 1.1 slice.22
  113.6 94.8 %all-gather.4.cloned.1.call-done = bf16[32768,256]{0,1:T(8,128)(2,1)} async-done(((bf16[2048,256]{0,1:T(8,128)(2,1)}), bf16[32768,256]{0,1:T(8,128)(2,1)}) %all-gather.4.cloned.1.call-update) | async-done | bytes 16777232 | tf_op jit(solution)/shard_map/all_gather | solution.py:32
  208.5 22.4 %copy.17 = bf16[32768,256]{1,0:T(8,128)(2,1)} copy(bf16[32768,256]{0,1:T(8,128)(2,1)} %all-gather.4.cloned.1.call-done) | data formatting | bytes 33554432
  230.9 93.5 %while.12 = (s32[]{:T(128)}, bf16[4,4,128,128]{3,2,1,0:T(8,128)(2,1)}, bf16[4,4,128,128]{3,2,1,0:T(8,128)(2,1)S(1)}, s32[4,4,16]{2,1,0:T(4,128)}, bf16[256,128,256]{2,1,0:T(8,128)(2,1)}, /*index=5*/s32[]{:T(128)}) while((s32[]{:T(128)}, bf16[4,4,128,128]{3,2,1,0:T(8,128)(2,1)}, bf16[4,4,128,128]{3,2,1,0:T(8,128)(2,1)S(1)}, ...), condition=%wide.region_5.6_spmd.clone.clone, body=%wide.region_0.5_spmd.clone.clone.sunk | while | flops 1625828864 | bytes 22169436 | solution.py:63
  231.7 8.5 %gather_fusion = bf16[64,128,256]{2,1,0:T(8,128)(2,1)} fusion(bf16[256,128,256]{2,1,0:T(8,128)(2,1)} %get-tuple-element.155, s32[1024]{0:T(1024)S(1)} %pad_clamp_fusion.2), kind=kCustom, calls=%fused_computation.clone.clone.1 | custom fusion | bytes 8388864 | tf_op jit(solution)/shard_map/while/body/eval_jaxpr/gather | solution.py:43
  240.2 2.9 fusion.146
  243.1 2.9 fusion.144
  246.0 3.8 %fusion.145 = f32[4,128,128]{2,1,0:T(8,128)S(1)} fusion(bf16[4,2048,256]{2,1,0:T(8,128)(2,1)} %bitcast.80, f32[4,128]{1,0:T(4,128)S(1)} %fusion.144, pred[128]{0:T(512)(128)(4,1)S(1)} %get-tuple-element.137, bf16[4,4,128,128]{3,2,1,0:T(8,128)(2,1)S(1)} %get-tuple-element.153, s32[]{:T(128)S(6)} %copy.22), kind=kOutput, calls=%fused_computation.25.clone.1 | convolution fusion | flops 541198848 | bytes 4590596 | tf_op jit(solution)/shard_map/while/body/eval_jaxpr/gqk,gkc->gqc/dot_general | solution.py:57
  249.8 4.5 %fusion.147 = bf16[4,4,128,128]{3,2,1,0:T(8,128)(2,1)} fusion(bf16[4,4,128,128]{3,2,1,0:T(8,128)(2,1)} %get-tuple-element.146, s32[]{:T(128)S(6)} %copy.22, f32[4,128,128]{2,1,0:T(8,128)S(1)} %fusion.145, bf16[4,2048,256]{2,1,0:T(8,128)(2,1)} %bitcast.81, f32[4,128]{1,0:T(4,128)S(1)} %fusion.146, pred[128]{0:T(512)(128)(4,1)S(1)} %get-tuple-element.138, ...), kind=kOutput, calls=%fused_computation.27.clone.1 | convolution fusion | flops 541329920 | bytes 4722688 | tf_op jit(solution)/shard_map/while/body/eval_jaxpr/gqk,gkc->gqc/dot_general | solution.py:57
  255.0 8.5 %gather_fusion = bf16[64,128,256]{2,1,0:T(8,128)(2,1)} fusion(bf16[256,128,256]{2,1,0:T(8,128)(2,1)} %get-tuple-element.155, s32[1024]{0:T(1024)S(1)} %pad_clamp_fusion.2), kind=kCustom, calls=%fused_computation.clone.clone.1 | custom fusion | bytes 8388864 | tf_op jit(solution)/shard_map/while/body/eval_jaxpr/gather | solution.py:43
  263.5 2.9 fusion.146
  266.4 2.9 fusion.144
  269.3 3.8 %fusion.145 = f32[4,128,128]{2,1,0:T(8,128)S(1)} fusion(bf16[4,2048,256]{2,1,0:T(8,128)(2,1)} %bitcast.80, f32[4,128]{1,0:T(4,128)S(1)} %fusion.144, pred[128]{0:T(512)(128)(4,1)S(1)} %get-tuple-element.137, bf16[4,4,128,128]{3,2,1,0:T(8,128)(2,1)S(1)} %get-tuple-element.153, s32[]{:T(128)S(6)} %copy.22), kind=kOutput, calls=%fused_computation.25.clone.1 | convolution fusion | flops 541198848 | bytes 4590596 | tf_op jit(solution)/shard_map/while/body/eval_jaxpr/gqk,gkc->gqc/dot_general | solution.py:57
  273.1 4.5 %fusion.147 = bf16[4,4,128,128]{3,2,1,0:T(8,128)(2,1)} fusion(bf16[4,4,128,128]{3,2,1,0:T(8,128)(2,1)} %get-tuple-element.146, s32[]{:T(128)S(6)} %copy.22, f32[4,128,128]{2,1,0:T(8,128)S(1)} %fusion.145, bf16[4,2048,256]{2,1,0:T(8,128)(2,1)} %bitcast.81, f32[4,128]{1,0:T(4,128)S(1)} %fusion.146, pred[128]{0:T(512)(128)(4,1)S(1)} %get-tuple-element.138, ...), kind=kOutput, calls=%fused_computation.27.clone.1 | convolution fusion | flops 541329920 | bytes 4722688 | tf_op jit(solution)/shard_map/while/body/eval_jaxpr/gqk,gkc->gqc/dot_general | solution.py:57
  278.4 8.5 %gather_fusion = bf16[64,128,256]{2,1,0:T(8,128)(2,1)} fusion(bf16[256,128,256]{2,1,0:T(8,128)(2,1)} %get-tuple-element.155, s32[1024]{0:T(1024)S(1)} %pad_clamp_fusion.2), kind=kCustom, calls=%fused_computation.clone.clone.1 | custom fusion | bytes 8388864 | tf_op jit(solution)/shard_map/while/body/eval_jaxpr/gather | solution.py:43
  286.9 2.9 fusion.146
  289.8 2.9 fusion.144
  292.7 3.8 %fusion.145 = f32[4,128,128]{2,1,0:T(8,128)S(1)} fusion(bf16[4,2048,256]{2,1,0:T(8,128)(2,1)} %bitcast.80, f32[4,128]{1,0:T(4,128)S(1)} %fusion.144, pred[128]{0:T(512)(128)(4,1)S(1)} %get-tuple-element.137, bf16[4,4,128,128]{3,2,1,0:T(8,128)(2,1)S(1)} %get-tuple-element.153, s32[]{:T(128)S(6)} %copy.22), kind=kOutput, calls=%fused_computation.25.clone.1 | convolution fusion | flops 541198848 | bytes 4590596 | tf_op jit(solution)/shard_map/while/body/eval_jaxpr/gqk,gkc->gqc/dot_general | solution.py:57
  296.5 4.5 %fusion.147 = bf16[4,4,128,128]{3,2,1,0:T(8,128)(2,1)} fusion(bf16[4,4,128,128]{3,2,1,0:T(8,128)(2,1)} %get-tuple-element.146, s32[]{:T(128)S(6)} %copy.22, f32[4,128,128]{2,1,0:T(8,128)S(1)} %fusion.145, bf16[4,2048,256]{2,1,0:T(8,128)(2,1)} %bitcast.81, f32[4,128]{1,0:T(4,128)S(1)} %fusion.146, pred[128]{0:T(512)(128)(4,1)S(1)} %get-tuple-element.138, ...), kind=kOutput, calls=%fused_computation.27.clone.1 | convolution fusion | flops 541329920 | bytes 4722688 | tf_op jit(solution)/shard_map/while/body/eval_jaxpr/gqk,gkc->gqc/dot_general | solution.py:57
  301.8 8.5 %gather_fusion = bf16[64,128,256]{2,1,0:T(8,128)(2,1)} fusion(bf16[256,128,256]{2,1,0:T(8,128)(2,1)} %get-tuple-element.155, s32[1024]{0:T(1024)S(1)} %pad_clamp_fusion.2), kind=kCustom, calls=%fused_computation.clone.clone.1 | custom fusion | bytes 8388864 | tf_op jit(solution)/shard_map/while/body/eval_jaxpr/gather | solution.py:43
  310.3 2.9 fusion.146
  313.2 2.9 fusion.144
  316.1 3.8 %fusion.145 = f32[4,128,128]{2,1,0:T(8,128)S(1)} fusion(bf16[4,2048,256]{2,1,0:T(8,128)(2,1)} %bitcast.80, f32[4,128]{1,0:T(4,128)S(1)} %fusion.144, pred[128]{0:T(512)(128)(4,1)S(1)} %get-tuple-element.137, bf16[4,4,128,128]{3,2,1,0:T(8,128)(2,1)S(1)} %get-tuple-element.153, s32[]{:T(128)S(6)} %copy.22), kind=kOutput, calls=%fused_computation.25.clone.1 | convolution fusion | flops 541198848 | bytes 4590596 | tf_op jit(solution)/shard_map/while/body/eval_jaxpr/gqk,gkc->gqc/dot_general | solution.py:57
  319.9 4.5 %fusion.147 = bf16[4,4,128,128]{3,2,1,0:T(8,128)(2,1)} fusion(bf16[4,4,128,128]{3,2,1,0:T(8,128)(2,1)} %get-tuple-element.146, s32[]{:T(128)S(6)} %copy.22, f32[4,128,128]{2,1,0:T(8,128)S(1)} %fusion.145, bf16[4,2048,256]{2,1,0:T(8,128)(2,1)} %bitcast.81, f32[4,128]{1,0:T(4,128)S(1)} %fusion.146, pred[128]{0:T(512)(128)(4,1)S(1)} %get-tuple-element.138, ...), kind=kOutput, calls=%fused_computation.27.clone.1 | convolution fusion | flops 541329920 | bytes 4722688 | tf_op jit(solution)/shard_map/while/body/eval_jaxpr/gqk,gkc->gqc/dot_general | solution.py:57
  324.4 14.3 %all_to_all.19 = bf16[8,256,128]{2,1,0:T(8,128)(2,1)S(1)} all-to-all(bf16[8,256,128]{2,1,0:T(8,128)(2,1)} %bitcast.88), channel_id=1, replica_groups=mesh['batch'=2,'head'=8,'blk'=16] {'head'}, dimensions={0} | all-to-all | bytes 1048576 | tf_op jit(solution)/shard_map/all_to_all | solution.py:65
  338.8 1.5 fusion.114
  (27 shorter events, 5.5 us)
Async XLA Ops:
  6.5 332.3 %copy-start = (bf16[1024,1024]{1,0:T(8,128)(2,1)S(1)}, bf16[1024,1024]{1,0:T(8,128)(2,1)}, u32[]{:S(2)}) copy-start(bf16[1024,1024]{1,0:T(8,128)(2,1)} %param.8) | copy-start | bytes 6291460
  6.5 99.5 %all-gather.6.cloned.1.call-start = ((), (), s32[]{:S(2)}) async-start(), calls=%async_computation.2 | async-start | bytes 4718592 | tf_op jit(solution)/shard_map/all_gather | solution.py:26
  7.3 201.2 %all-gather.4.cloned.1.call-start = ((), (), s32[]{:S(2)}) async-start(), calls=%async_computation.1 | async-start | bytes 17825792 | tf_op jit(solution)/shard_map/all_gather | solution.py:32
  110.0 1.2 copy-start.1
Sparse Core Ops, SparseCore 0:
  9.1 96.8 all-gather.5
  112.4 96.0 all-gather.3
where the time goes:
time: 349 us; the launch traced here: 347 us
  waiting for transfers between devices  191 us (55%)
  local copies, waits for them, and re-layouts  64.1 us (18%)
  matrix products  61.8 us (18%)
  blocking collectives  14.3 us (4%)
  between operations  13.5 us (4%)
    all_gather x1, waiting for transfers between devices, on_device(): lax.all_gather(own_rows, 'head', axis=0, tiled=True)  95.1 us
    all_gather x1, waiting for transfers between devices, on_device(): source = lax.all_gather(key_value, 'blk', axis=0, tiled=True)  94.8 us
    gather x4, local copies, waits for them, and re-layouts, attend(): source_blocks[positions].reshape(group_size, KSEL * BLK, 2 * head_width)  34 us
    dot_general x8, matrix products, attend(): jnp.einsum('gqk,gkc->gqc', weights, value_rows, preferred_element_type=jn...  33.1 us
    unnamed x7, local copies, waits for them, and re-layouts  25 us
    sub x8, matrix products, attend(): raised = jnp.exp(scores - row_max)  23.2 us
    all_to_all x1, blocking collectives, on_device(): lax.all_to_all(attended, 'head', split_axis=0, concat_axis=1, tiled=True)  14.3 us
  transfers between devices with their start and end apart: 2, of which 2 were waited for; matrix products, arithmetic and copies ran while one was open for 1% of the time, Pallas kernels for 0%

commit v1 on v0

--- a/solution.py
+++ b/solution.py
@@ -13,6 +13,11 @@
 
 
 def on_device(tokens, proj_weight, out_weight, pattern):
+
+    def rest_flows_up(x_part):
+        t_next = lax.all_to_all(jnp.stack(lax.axis_size("head") * [x_part], axis=0), "head", 0, 0)
+        return jnp.concatenate(t_next, axis=0)
+
     heads_axis = lax.axis_size("head")
     local_heads = H // heads_axis
     head_width = local_heads * HD
@@ -23,9 +28,7 @@
     columns = lax.dynamic_slice_in_dim(proj_weight, start_col, col_width, 1)
     columns = columns.reshape(D, local_heads, 3, HD).transpose(0, 2, 1, 3).reshape(D, col_width)
     projected = jnp.dot(
-        lax.all_gather(own_rows, "head", axis=0, tiled=True),
-        columns,
-        preferred_element_type=jnp.float32,
+        rest_flows_up(own_rows), columns, preferred_element_type=jnp.float32
     ).astype(jnp.bfloat16)
     queries = projected[:, :head_width]
     key_value = projected[:, head_width:]

time: 349 us -> 309 us (0.89)
  waiting for transfers between devices: 191 us -> 142 us
  starting transfers between devices: 0.04 us -> 5.98 us
  local copies, waits for them, and re-layouts: 64.1 us -> 67.9 us
    all_gather x1 -> x0, waiting for transfers between devices: 95.1 us -> none  [on_device(): lax.all_gather(own_rows, 'head', axis=0, tiled=True)]
    all_to_all x0 -> x1, waiting for transfers between devices: none -> 44.1 us  [rest_flows_up(): lax.all_to_all(jnp.stack(lax.axis_size('head') * [x_part], axis=0), 'head...]
    all_to_all x0 -> x1, starting transfers between devices: none -> 5.95 us  [rest_flows_up(): lax.all_to_all(jnp.stack(lax.axis_size('head') * [x_part], axis=0), 'head...]
    another operation x0 -> x1, local copies, waits for them, and re-layouts: none -> 3.7 us  [rest_flows_up(): jnp.stack(lax.axis_size('head') * [x_part], axis=0)]
  transfers between devices with their start and end apart: 2 -> 2, of which waited for: 2 -> 2; matrix products, arithmetic and copies ran while one was open for 1% -> 2% of each run, Pallas kernels for 0% -> 0%
where the time goes in v1:
time: 309 us; the launch traced here: 308 us
  waiting for transfers between devices  142 us (46%)
  local copies, waits for them, and re-layouts  67.9 us (22%)
  matrix products  61.8 us (20%)
  blocking collectives  14.3 us (5%)
  between operations  13.5 us (4%)
  starting transfers between devices  5.98 us (2%)
    all_gather x1, waiting for transfers between devices, on_device(): source = lax.all_gather(key_value, 'blk', axis=0, tiled=True)  97.5 us
    all_to_all x1, waiting for transfers between devices, rest_flows_up(): lax.all_to_all(jnp.stack(lax.axis_size('head') * [x_part], axis=0), 'head...  44.1 us
    gather x4, local copies, waits for them, and re-layouts, attend(): source_blocks[positions].reshape(group_size, KSEL * BLK, 2 * head_width)  34 us
    dot_general x8, matrix products, attend(): jnp.einsum('gqk,gkc->gqc', weights, value_rows, preferred_element_type=jn...  33.1 us
    unnamed x7, local copies, waits for them, and re-layouts  25.1 us
    sub x8, matrix products, attend(): raised = jnp.exp(scores - row_max)  23.2 us
    all_to_all x1, blocking collectives, on_device(): lax.all_to_all(attended, 'head', split_axis=0, concat_axis=1, tiled=True)  14.3 us
  transfers between devices with their start and end apart: 2, of which 2 were waited for; matrix products, arithmetic and copies ran while one was open for 2% of the time, Pallas kernels for 0%

profile of v1, /device:TPU:1, one launch (start us, length us, event | category | flops | bytes accessed | tf_op | source)
XLA Modules:
  0.0 307.9 jit_solution(15817231137070274681)
XLA Ops:
  6.5 3.7 %stack.3 = bf16[8,256,1024]{2,1,0:T(8,128)(2,1)} broadcast(bf16[256,1024]{1,0:T(8,128)(2,1)} %bitcast.83), dimensions={1,2} | broadcast | bytes 4718592 | tf_op jit(solution)/shard_map/stack | solution.py:18
  10.2 5.9 %all-to-all-start = ((bf16[8,256,1024]{2,1,0:T(8,128)(2,1)}), bf16[8,256,1024]{2,1,0:T(8,128)(2,1)}, u32[]{:S(2)}, u32[]{:S(2)}) async-start(bf16[8,256,1024]{2,1,0:T(8,128)(2,1)} %stack.3), calls=%async_computation | async-start | bytes 8388608 | tf_op jit(solution)/shard_map/all_to_all | solution.py:18
  16.2 1.2 constant_dynamic-slice_fusion
  17.5 1.2 copy.18
  18.7 1.2 copy.12
  19.9 44.1 %all-to-all-done = bf16[8,256,1024]{2,1,0:T(8,128)(2,1)} async-done(((bf16[8,256,1024]{2,1,0:T(8,128)(2,1)}), bf16[8,256,1024]{2,1,0:T(8,128)(2,1)}, u32[]{:S(2)}, u32[]{:S(2)}) %all-to-all-start) | async-done | bytes 4194336 | tf_op jit(solution)/shard_map/all_to_all | solution.py:18
  64.0 4.0 %fusion.106 = bf16[2048,384]{0,1:T(8,128)(2,1)S(1)} fusion(bf16[1024,384]{0,1:T(8,128)(2,1)S(1)} %bitcast.82, bf16[2048,1024]{1,0:T(8,128)(2,1)} %bitcast.4), kind=kOutput, calls=%fused_computation.65 | convolution fusion | flops 1611399168 | bytes 6553600 | tf_op jit(solution)/shard_map/dot_general | solution.py:30
  71.6 97.5 %all-gather.2.cloned.1.call-done = bf16[32768,256]{0,1:T(8,128)(2,1)} async-done(((bf16[2048,256]{0,1:T(8,128)(2,1)}), bf16[32768,256]{0,1:T(8,128)(2,1)}) %all-gather.2.cloned.1.call-update) | async-done | bytes 16777232 | tf_op jit(solution)/shard_map/all_gather | solution.py:35
  169.2 22.4 %copy.17 = bf16[32768,256]{1,0:T(8,128)(2,1)} copy(bf16[32768,256]{0,1:T(8,128)(2,1)} %all-gather.2.cloned.1.call-done) | data formatting | bytes 33554432
  191.6 93.5 %while.12 = (s32[]{:T(128)}, bf16[4,4,128,128]{3,2,1,0:T(8,128)(2,1)}, bf16[4,4,128,128]{3,2,1,0:T(8,128)(2,1)S(1)}, s32[4,4,16]{2,1,0:T(4,128)}, bf16[256,128,256]{2,1,0:T(8,128)(2,1)}, /*index=5*/s32[]{:T(128)}) while((s32[]{:T(128)}, bf16[4,4,128,128]{3,2,1,0:T(8,128)(2,1)}, bf16[4,4,128,128]{3,2,1,0:T(8,128)(2,1)S(1)}, ...), condition=%wide.region_5.6_spmd.clone.clone, body=%wide.region_0.5_spmd.clone.clone.sunk | while | flops 1625828864 | bytes 22169436 | solution.py:66
  192.4 8.5 %gather_fusion = bf16[64,128,256]{2,1,0:T(8,128)(2,1)} fusion(bf16[256,128,256]{2,1,0:T(8,128)(2,1)} %get-tuple-element.155, s32[1024]{0:T(1024)S(1)} %pad_clamp_fusion.2), kind=kCustom, calls=%fused_computation.clone.clone.1 | custom fusion | bytes 8388864 | tf_op jit(solution)/shard_map/while/body/eval_jaxpr/gather | solution.py:46
  200.9 2.9 fusion.140
  203.8 2.9 fusion.138
  206.7 3.8 %fusion.139 = f32[4,128,128]{2,1,0:T(8,128)S(1)} fusion(bf16[4,2048,256]{2,1,0:T(8,128)(2,1)} %bitcast.76, f32[4,128]{1,0:T(4,128)S(1)} %fusion.138, pred[128]{0:T(512)(128)(4,1)S(1)} %get-tuple-element.137, bf16[4,4,128,128]{3,2,1,0:T(8,128)(2,1)S(1)} %get-tuple-element.153, s32[]{:T(128)S(6)} %copy.22), kind=kOutput, calls=%fused_computation.25.clone.1 | convolution fusion | flops 541198848 | bytes 4590596 | tf_op jit(solution)/shard_map/while/body/eval_jaxpr/gqk,gkc->gqc/dot_general | solution.py:60
  210.5 4.5 %fusion.141 = bf16[4,4,128,128]{3,2,1,0:T(8,128)(2,1)} fusion(bf16[4,4,128,128]{3,2,1,0:T(8,128)(2,1)} %get-tuple-element.146, s32[]{:T(128)S(6)} %copy.22, f32[4,128,128]{2,1,0:T(8,128)S(1)} %fusion.139, bf16[4,2048,256]{2,1,0:T(8,128)(2,1)} %bitcast.77, f32[4,128]{1,0:T(4,128)S(1)} %fusion.140, pred[128]{0:T(512)(128)(4,1)S(1)} %get-tuple-element.138, ...), kind=kOutput, calls=%fused_computation.27.clone.1 | convolution fusion | flops 541329920 | bytes 4722688 | tf_op jit(solution)/shard_map/while/body/eval_jaxpr/gqk,gkc->gqc/dot_general | solution.py:60
  215.7 8.5 %gather_fusion = bf16[64,128,256]{2,1,0:T(8,128)(2,1)} fusion(bf16[256,128,256]{2,1,0:T(8,128)(2,1)} %get-tuple-element.155, s32[1024]{0:T(1024)S(1)} %pad_clamp_fusion.2), kind=kCustom, calls=%fused_computation.clone.clone.1 | custom fusion | bytes 8388864 | tf_op jit(solution)/shard_map/while/body/eval_jaxpr/gather | solution.py:46
  224.3 2.9 fusion.140
  227.2 2.9 fusion.138
  230.1 3.8 %fusion.139 = f32[4,128,128]{2,1,0:T(8,128)S(1)} fusion(bf16[4,2048,256]{2,1,0:T(8,128)(2,1)} %bitcast.76, f32[4,128]{1,0:T(4,128)S(1)} %fusion.138, pred[128]{0:T(512)(128)(4,1)S(1)} %get-tuple-element.137, bf16[4,4,128,128]{3,2,1,0:T(8,128)(2,1)S(1)} %get-tuple-element.153, s32[]{:T(128)S(6)} %copy.22), kind=kOutput, calls=%fused_computation.25.clone.1 | convolution fusion | flops 541198848 | bytes 4590596 | tf_op jit(solution)/shard_map/while/body/eval_jaxpr/gqk,gkc->gqc/dot_general | solution.py:60
  233.9 4.5 %fusion.141 = bf16[4,4,128,128]{3,2,1,0:T(8,128)(2,1)} fusion(bf16[4,4,128,128]{3,2,1,0:T(8,128)(2,1)} %get-tuple-element.146, s32[]{:T(128)S(6)} %copy.22, f32[4,128,128]{2,1,0:T(8,128)S(1)} %fusion.139, bf16[4,2048,256]{2,1,0:T(8,128)(2,1)} %bitcast.77, f32[4,128]{1,0:T(4,128)S(1)} %fusion.140, pred[128]{0:T(512)(128)(4,1)S(1)} %get-tuple-element.138, ...), kind=kOutput, calls=%fused_computation.27.clone.1 | convolution fusion | flops 541329920 | bytes 4722688 | tf_op jit(solution)/shard_map/while/body/eval_jaxpr/gqk,gkc->gqc/dot_general | solution.py:60
  239.1 8.5 %gather_fusion = bf16[64,128,256]{2,1,0:T(8,128)(2,1)} fusion(bf16[256,128,256]{2,1,0:T(8,128)(2,1)} %get-tuple-element.155, s32[1024]{0:T(1024)S(1)} %pad_clamp_fusion.2), kind=kCustom, calls=%fused_computation.clone.clone.1 | custom fusion | bytes 8388864 | tf_op jit(solution)/shard_map/while/body/eval_jaxpr/gather | solution.py:46
  247.6 2.9 fusion.140
  250.5 2.9 fusion.138
  253.4 3.8 %fusion.139 = f32[4,128,128]{2,1,0:T(8,128)S(1)} fusion(bf16[4,2048,256]{2,1,0:T(8,128)(2,1)} %bitcast.76, f32[4,128]{1,0:T(4,128)S(1)} %fusion.138, pred[128]{0:T(512)(128)(4,1)S(1)} %get-tuple-element.137, bf16[4,4,128,128]{3,2,1,0:T(8,128)(2,1)S(1)} %get-tuple-element.153, s32[]{:T(128)S(6)} %copy.22), kind=kOutput, calls=%fused_computation.25.clone.1 | convolution fusion | flops 541198848 | bytes 4590596 | tf_op jit(solution)/shard_map/while/body/eval_jaxpr/gqk,gkc->gqc/dot_general | solution.py:60
  257.2 4.5 %fusion.141 = bf16[4,4,128,128]{3,2,1,0:T(8,128)(2,1)} fusion(bf16[4,4,128,128]{3,2,1,0:T(8,128)(2,1)} %get-tuple-element.146, s32[]{:T(128)S(6)} %copy.22, f32[4,128,128]{2,1,0:T(8,128)S(1)} %fusion.139, bf16[4,2048,256]{2,1,0:T(8,128)(2,1)} %bitcast.77, f32[4,128]{1,0:T(4,128)S(1)} %fusion.140, pred[128]{0:T(512)(128)(4,1)S(1)} %get-tuple-element.138, ...), kind=kOutput, calls=%fused_computation.27.clone.1 | convolution fusion | flops 541329920 | bytes 4722688 | tf_op jit(solution)/shard_map/while/body/eval_jaxpr/gqk,gkc->gqc/dot_general | solution.py:60
  262.5 8.5 %gather_fusion = bf16[64,128,256]{2,1,0:T(8,128)(2,1)} fusion(bf16[256,128,256]{2,1,0:T(8,128)(2,1)} %get-tuple-element.155, s32[1024]{0:T(1024)S(1)} %pad_clamp_fusion.2), kind=kCustom, calls=%fused_computation.clone.clone.1 | custom fusion | bytes 8388864 | tf_op jit(solution)/shard_map/while/body/eval_jaxpr/gather | solution.py:46
  271.0 2.9 fusion.140
  273.9 2.9 fusion.138
  276.8 3.8 %fusion.139 = f32[4,128,128]{2,1,0:T(8,128)S(1)} fusion(bf16[4,2048,256]{2,1,0:T(8,128)(2,1)} %bitcast.76, f32[4,128]{1,0:T(4,128)S(1)} %fusion.138, pred[128]{0:T(512)(128)(4,1)S(1)} %get-tuple-element.137, bf16[4,4,128,128]{3,2,1,0:T(8,128)(2,1)S(1)} %get-tuple-element.153, s32[]{:T(128)S(6)} %copy.22), kind=kOutput, calls=%fused_computation.25.clone.1 | convolution fusion | flops 541198848 | bytes 4590596 | tf_op jit(solution)/shard_map/while/body/eval_jaxpr/gqk,gkc->gqc/dot_general | solution.py:60
  280.6 4.5 %fusion.141 = bf16[4,4,128,128]{3,2,1,0:T(8,128)(2,1)} fusion(bf16[4,4,128,128]{3,2,1,0:T(8,128)(2,1)} %get-tuple-element.146, s32[]{:T(128)S(6)} %copy.22, f32[4,128,128]{2,1,0:T(8,128)S(1)} %fusion.139, bf16[4,2048,256]{2,1,0:T(8,128)(2,1)} %bitcast.77, f32[4,128]{1,0:T(4,128)S(1)} %fusion.140, pred[128]{0:T(512)(128)(4,1)S(1)} %get-tuple-element.138, ...), kind=kOutput, calls=%fused_computation.27.clone.1 | convolution fusion | flops 541329920 | bytes 4722688 | tf_op jit(solution)/shard_map/while/body/eval_jaxpr/gqk,gkc->gqc/dot_general | solution.py:60
  285.1 14.3 %all_to_all.24 = bf16[8,256,128]{2,1,0:T(8,128)(2,1)S(1)} all-to-all(bf16[8,256,128]{2,1,0:T(8,128)(2,1)} %bitcast.85), channel_id=1, replica_groups=mesh['batch'=2,'head'=8,'blk'=16] {'head'}, dimensions={0} | all-to-all | bytes 1048576 | tf_op jit(solution)/shard_map/all_to_all | solution.py:68
  299.6 1.5 fusion.107
  (27 shorter events, 7.0 us)
Async XLA Ops:
  6.5 293.0 %copy-start = (bf16[1024,1024]{1,0:T(8,128)(2,1)S(1)}, bf16[1024,1024]{1,0:T(8,128)(2,1)}, u32[]{:S(2)}) copy-start(bf16[1024,1024]{1,0:T(8,128)(2,1)} %param.8) | copy-start | bytes 6291460
  10.2 53.8 %all-to-all-start = ((bf16[8,256,1024]{2,1,0:T(8,128)(2,1)}), bf16[8,256,1024]{2,1,0:T(8,128)(2,1)}, u32[]{:S(2)}, u32[]{:S(2)}) async-start(bf16[8,256,1024]{2,1,0:T(8,128)(2,1)} %stack.3), calls=%async_computation | async-start | bytes 8388608 | tf_op jit(solution)/shard_map/all_to_all | solution.py:18
  16.2 153.0 %all-gather.2.cloned.1.call-start = ((), (), s32[]{:S(2)}) async-start(), calls=%async_computation.2 | async-start | bytes 17825792 | tf_op jit(solution)/shard_map/all_gather | solution.py:35
  68.0 1.2 copy-start.1
Sparse Core Ops, SparseCore 0:
  70.4 98.7 all-gather.1
